TPU v7x, 32 devices: a whole 2x2x4 slice. The times are simulated.
32 devices in a mesh: shard: 2 (over y), ctx: 4 (over x, core), tensor: 4 (over z).
Axes of the slice: x: 2, y: 2, z: 4, core: 2. Of those that a mesh axis runs over, the one named last changes fastest.
Arguments:
- inputs: bfloat16 [2, 1024, 2048], P('shard', 'ctx'), may hold values from -6 to 6
- cotangent: bfloat16 [2, 1024, 2048], P('shard', 'ctx'), may hold values from -6 to 6
- piece_starts: int32 [2, 3], P('shard'), may hold values from 0 to 768, as said below
- positions: int32 [2, 1024], P('shard', 'ctx'), may hold values from 0 to 303, as said below
- w_qkv: float32 [2048, 8, 768], P(('shard', 'ctx'), 'tensor'), may hold values from -0.125 to 0.125
- b_qkv: float32 [8, 768], P('tensor'), may hold values from -1.2 to 1.2
- w_dense: float32 [2048, 8, 256], P(('shard', 'ctx'), 'tensor'), may hold values from -0.5 to 0.5
- w_fc1: float32 [2048, 8192], P(('shard', 'ctx'), 'tensor'), may hold values from -0.125 to 0.125
- b_fc1: float32 [8192], P('tensor'), may hold values from -3 to 3
- w_fc2: float32 [2048, 8192], P(('shard', 'ctx'), 'tensor'), may hold values from -0.0625 to 0.0625
- out_bias: float32 [2048], replicated, may hold values from -3 to 3
- ln1_gain: float32 [2048], replicated, may hold values from 0.1 to 1.9
- ln1_bias: float32 [2048], replicated, may hold values from -2 to 2
- ln2_gain: float32 [2048], replicated, may hold values from 0.1 to 1.9
- ln2_bias: float32 [2048], replicated, may hold values from -2 to 2
Outputs:
- output: bfloat16 [2, 1024, 2048], P('shard', 'ctx')
- grad_inputs: float32 [2, 1024, 2048], P('shard', 'ctx')
- grad_w_qkv: float32 [2048, 8, 768], P(('shard', 'ctx'), 'tensor')
- grad_b_qkv: float32 [8, 768], P('tensor')
- grad_w_dense: float32 [2048, 8, 256], P(('shard', 'ctx'), 'tensor')
- grad_w_fc1: float32 [2048, 8192], P(('shard', 'ctx'), 'tensor')
- grad_b_fc1: float32 [8192], P('tensor')
- grad_w_fc2: float32 [2048, 8192], P(('shard', 'ctx'), 'tensor')
- grad_out_bias: float32 [2048], replicated
- grad_ln1_gain: float32 [2048], replicated
- grad_ln1_bias: float32 [2048], replicated
- grad_ln2_gain: float32 [2048], replicated
- grad_ln2_bias: float32 [2048], replicated
Inputs may be any that keep to these rules, and one draw needn't show every extreme that they name: `piece_starts`: for each sequence, 3 starts in increasing order; its picture pieces of 256 tokens do not intersect and lie inside the sequence. `positions`: in each sequence the position starts at 0 and rises by one at every token outside the picture pieces and at the first of every 16 tokens of a piece; the other tokens of a piece keep the position before them.
All inputs are finite; a program needn't handle non-finite values.
Results may differ from a plain program's by a relative error of at most 0.012.
Values may be sent and summed in bfloat16 or wider, within the bound.
No kernel may reach another device: no remote copies, remote signals or barrier semaphores. Data moves between devices by JAX's collectives and lax.ppermute only.
A program may use at most 256 MiB of HBM per device.

v0:
```python
import jax
import jax.numpy as jnp
from jax import lax
from jax.sharding import PartitionSpec as P

HEAD = 256
ROT = 64
PIECE = 256
PIECES = 3
EPSILON = 1e-05
ROPE_BASE = 10000.0


def layer_norm(values, norm_gain, norm_shift):
    centred = values - jnp.mean(values, axis=-1, keepdims=True)
    spread = jnp.mean(centred * centred, axis=-1, keepdims=True)
    return centred * lax.rsqrt(spread + EPSILON) * norm_gain + norm_shift


def rotary_tables(places):
    half_rot = ROT // 2
    frequency = ROPE_BASE ** (-(jnp.arange(half_rot, dtype=jnp.float32) * 2.0) / ROT)
    angles = places.astype(jnp.float32)[..., None] * frequency
    angles = jnp.concatenate([angles, angles], axis=-1)
    return (jnp.cos(angles)[..., None, :], jnp.sin(angles)[..., None, :])


def rotate(head_values, cosine, sine_part):
    half_rot = ROT // 2
    rotated_part = head_values[..., :ROT]
    turned = jnp.concatenate([-rotated_part[..., half_rot:], rotated_part[..., :half_rot]], axis=-1)
    return jnp.concatenate(
        [rotated_part * cosine + turned * sine_part, head_values[..., ROT:]], axis=-1
    )


def piece_map(token_index, starts):
    inside = (token_index[None, :, None] >= starts[:, None, :]) & (
        token_index[None, :, None] < starts[:, None, :] + PIECE
    )
    labels = jnp.arange(1, PIECES + 1, dtype=jnp.int32)
    return jnp.sum(jnp.where(inside, labels, 0), axis=2)


def exact_gelu(pre_act):
    return jax.nn.gelu(pre_act, approximate=False)


def cross_rows(left_rows, right_rows):
    return lax.dot_general(
        left_rows, right_rows, (((1,), (1,)), ((), ())), preferred_element_type=jnp.float32
    )


def outer_rows(left_rows, right_rows):
    return lax.dot_general(
        left_rows, right_rows, (((0,), (0,)), ((), ())), preferred_element_type=jnp.float32
    )


def local(
    inputs,
    cotangent,
    piece_starts,
    positions,
    w_qkv,
    b_qkv,
    w_dense,
    w_fc1,
    b_fc1,
    w_fc2,
    out_bias,
    ln1_gain,
    ln1_bias,
    ln2_gain,
    ln2_bias,
):
    groups, seq_span, model_width = inputs.shape
    row_count = groups * seq_span
    local_heads = w_qkv.shape[1]
    shard_rows = w_qkv.shape[0]
    seq_length = seq_span * lax.axis_size("ctx")
    score_scale = HEAD ** (-0.5)
    attn_cols = local_heads * HEAD
    joint_cols = local_heads * 3 * HEAD
    residual = inputs.astype(jnp.float32).reshape(row_count, model_width)
    normed_one = layer_norm(residual, ln1_gain, ln1_bias).astype(jnp.bfloat16)
    normed_two = layer_norm(residual, ln2_gain, ln2_bias).astype(jnp.bfloat16)
    qkv_low = w_qkv.astype(jnp.bfloat16)
    dense_low = w_dense.astype(jnp.bfloat16)
    fc1_low = w_fc1.astype(jnp.bfloat16)
    fc2_low = w_fc2.astype(jnp.bfloat16)
    front_qkv, front_fc1 = (
        lax.all_gather(qkv_low, ("shard", "ctx"), axis=0, tiled=True),
        lax.all_gather(fc1_low, ("shard", "ctx"), axis=0, tiled=True),
    )
    joined = jnp.dot(
        normed_one, front_qkv.reshape(model_width, joint_cols), preferred_element_type=jnp.float32
    )
    inner_sum = jnp.dot(normed_two, front_fc1, preferred_element_type=jnp.float32)
    joined = joined.reshape(groups, seq_span, local_heads, 3 * HEAD) + b_qkv
    cosine, sine_part = rotary_tables(positions)
    queries = rotate(joined[..., :HEAD], cosine, sine_part).astype(jnp.bfloat16)
    key_rows = rotate(joined[..., HEAD : 2 * HEAD], cosine, sine_part).astype(jnp.bfloat16)
    value_rows = joined[..., 2 * HEAD :].astype(jnp.bfloat16)
    all_keys, all_values = (
        lax.all_gather(key_rows, "ctx", axis=1, tiled=True),
        lax.all_gather(value_rows, "ctx", axis=1, tiled=True),
    )
    key_index = jnp.arange(seq_length, dtype=jnp.int32)
    query_index = lax.axis_index("ctx") * seq_span + jnp.arange(seq_span, dtype=jnp.int32)
    key_piece = piece_map(key_index, piece_starts)
    query_piece = piece_map(query_index, piece_starts)
    allowed = (key_index[None, None, :] <= query_index[None, :, None]) | (
        key_piece[:, None, :] == query_piece[:, :, None]
    ) & (query_piece[:, :, None] > 0)

    def score_block(query_low):
        raw_scores = (
            jnp.einsum("gqhd,gkhd->ghqk", query_low, all_keys, preferred_element_type=jnp.float32)
            * score_scale
        )
        return jnp.where(allowed[:, None], raw_scores, -1e30)

    scores = score_block(queries)
    row_max = jnp.max(scores, axis=-1, keepdims=True)
    exponent = jnp.exp(scores - row_max)
    row_total = jnp.sum(exponent, axis=-1, keepdims=True)
    weights = exponent / row_total
    log_total = row_max + jnp.log(row_total)
    attended = jnp.einsum(
        "ghqk,gkhd->gqhd",
        weights.astype(jnp.bfloat16),
        all_values,
        preferred_element_type=jnp.float32,
    )
    context = attended.reshape(row_count, attn_cols).astype(jnp.bfloat16)
    pre_gelu = inner_sum + b_fc1
    hidden = exact_gelu(pre_gelu).astype(jnp.bfloat16)
    piece_pair = (
        lax.all_gather(dense_low, ("shard", "ctx"), axis=0, tiled=True),
        lax.all_gather(fc2_low, ("shard", "ctx"), axis=0, tiled=True),
    )
    row_span = piece_pair[0].shape[0]
    block_out = cross_rows(context, piece_pair[0].reshape(row_span, attn_cols)) + cross_rows(
        hidden, piece_pair[1]
    )
    summed_out = lax.psum(block_out, "tensor")
    output = (
        (residual + summed_out + out_bias)
        .astype(jnp.bfloat16)
        .reshape(groups, seq_span, model_width)
    )
    grad_low = cotangent.reshape(row_count, model_width)
    grad_flat = grad_low.astype(jnp.float32)
    back_dense, back_fc2 = (
        lax.all_gather(dense_low, ("shard", "ctx"), axis=0, tiled=True),
        lax.all_gather(fc2_low, ("shard", "ctx"), axis=0, tiled=True),
    )
    grad_context = jnp.dot(
        grad_low, back_dense.reshape(model_width, attn_cols), preferred_element_type=jnp.float32
    )
    grad_hidden = jnp.dot(grad_low, back_fc2, preferred_element_type=jnp.float32)
    outer_sum = lax.psum_scatter(
        jnp.concatenate([outer_rows(grad_low, context), outer_rows(grad_low, hidden)], axis=1),
        ("shard", "ctx"),
        scatter_dimension=0,
        tiled=True,
    )
    grad_w_dense = outer_sum[:, :attn_cols].reshape(shard_rows, local_heads, HEAD)
    grad_w_fc2 = outer_sum[:, attn_cols:]
    gelu_value, gelu_back = jax.vjp(exact_gelu, pre_gelu)
    grad_inner = gelu_back(grad_hidden)[0].astype(jnp.bfloat16)
    grad_mixed = grad_context.astype(jnp.bfloat16).reshape(groups, seq_span, local_heads, HEAD)
    probs_again = jnp.exp(score_block(queries) - log_total)
    grad_probs = jnp.einsum(
        "gqhd,gkhd->ghqk", grad_mixed, all_values, preferred_element_type=jnp.float32
    )
    centre = jnp.sum(probs_again * grad_probs, axis=-1, keepdims=True)
    grad_scores = (probs_again * (grad_probs - centre)).astype(jnp.bfloat16)
    grad_queries = (
        jnp.einsum("ghqk,gkhd->gqhd", grad_scores, all_keys, preferred_element_type=jnp.float32)
        * score_scale
    )
    key_terms = (
        jnp.einsum("ghqk,gqhd->gkhd", grad_scores, queries, preferred_element_type=jnp.float32)
        * score_scale
    )
    value_terms = jnp.einsum(
        "ghqk,gqhd->gkhd",
        probs_again.astype(jnp.bfloat16),
        grad_mixed,
        preferred_element_type=jnp.float32,
    )
    grad_keys, grad_values = (
        lax.psum_scatter(key_terms, "ctx", scatter_dimension=1, tiled=True),
        lax.psum_scatter(value_terms, "ctx", scatter_dimension=1, tiled=True),
    )
    back_query = rotate(grad_queries, cosine, -sine_part)
    back_key = rotate(grad_keys, cosine, -sine_part)
    grad_joined = (
        jnp.concatenate([back_query, back_key, grad_values], axis=-1)
        .reshape(row_count, joint_cols)
        .astype(jnp.bfloat16)
    )
    piece_pair = (
        lax.all_gather(qkv_low, ("shard", "ctx"), axis=0, tiled=True),
        lax.all_gather(fc1_low, ("shard", "ctx"), axis=0, tiled=True),
    )
    row_span = piece_pair[0].shape[0]
    block_one = cross_rows(grad_joined, piece_pair[0].reshape(row_span, joint_cols))
    block_two = cross_rows(grad_inner, piece_pair[1])
    grad_norm_one = block_one
    grad_norm_two = block_two
    inner_grads = lax.psum_scatter(
        jnp.concatenate(
            [outer_rows(normed_one, grad_joined), outer_rows(normed_two, grad_inner)], axis=1
        ),
        ("shard", "ctx"),
        scatter_dimension=0,
        tiled=True,
    )
    grad_w_qkv = inner_grads[:, :joint_cols].reshape(shard_rows, local_heads, 3 * HEAD)
    grad_w_fc1 = inner_grads[:, joint_cols:]
    grad_norm_one, grad_norm_two = lax.psum((grad_norm_one, grad_norm_two), "tensor")
    norm_value_one, norm_back_one = jax.vjp(layer_norm, residual, ln1_gain, ln1_bias)
    norm_value_two, norm_back_two = jax.vjp(layer_norm, residual, ln2_gain, ln2_bias)
    grad_res_one, grad_gain_one, grad_shift_one = norm_back_one(grad_norm_one)
    grad_res_two, grad_gain_two, grad_shift_two = norm_back_two(grad_norm_two)
    grad_inputs = (grad_flat + grad_res_one + grad_res_two).reshape(groups, seq_span, model_width)
    bias_qkv_term = jnp.sum(grad_joined.astype(jnp.float32), axis=0).reshape(local_heads, 3 * HEAD)
    bias_fc1_term = jnp.sum(grad_inner.astype(jnp.float32), axis=0)
    small_sums = lax.psum(
        (
            bias_qkv_term,
            bias_fc1_term,
            jnp.sum(grad_flat, axis=0),
            grad_gain_one,
            grad_shift_one,
            grad_gain_two,
            grad_shift_two,
        ),
        ("shard", "ctx"),
    )
    return (
        output,
        grad_inputs,
        grad_w_qkv,
        small_sums[0],
        grad_w_dense,
        grad_w_fc1,
        small_sums[1],
        grad_w_fc2,
        small_sums[2],
        small_sums[3],
        small_sums[4],
        small_sums[5],
        small_sums[6],
    )


def solution(mesh):
    in_specs = (
        P("shard", "ctx", None),
        P("shard", "ctx", None),
        P("shard", None),
        P("shard", "ctx"),
        P(("shard", "ctx"), "tensor", None),
        P("tensor", None),
        P(("shard", "ctx"), "tensor", None),
        P(("shard", "ctx"), "tensor"),
        P("tensor"),
        P(("shard", "ctx"), "tensor"),
        P(),
        P(),
        P(),
        P(),
        P(),
    )
    out_specs = (
        P("shard", "ctx", None),
        P("shard", "ctx", None),
        P(("shard", "ctx"), "tensor", None),
        P("tensor", None),
        P(("shard", "ctx"), "tensor", None),
        P(("shard", "ctx"), "tensor"),
        P("tensor"),
        P(("shard", "ctx"), "tensor"),
        P(),
        P(),
        P(),
        P(),
        P(),
    )
    return jax.shard_map(local, mesh=mesh, in_specs=in_specs, out_specs=out_specs, check_vma=False)
```

profile of v0, /device:TPU:0, one launch (start us, length us, event | category | flops | bytes accessed | tf_op | source)
XLA Modules:
  0.0 868.9 jit_solution(4241122452107551407)
XLA Ops:
  7.3 2.9 convert_element_type.123
  13.3 45.3 %all-gather.7.cloned.1.call-done = bf16[2048,2,768]{2,1,0:T(2,128)(2,1)} async-done(((bf16[256,2,768]{2,1,0:T(2,128)(2,1)}), bf16[2048,2,768]{2,1,0:T(2,128)(2,1)}) %all-gather.7.cloned.1.call-update) | async-done | bytes 6291472 | tf_op jit(solution)/shard_map/all_gather | solution.py:94
  58.6 6.8 copy.109
  65.4 8.8 %copy.74 = bf16[2048,1536]{0,1:T(8,128)(2,1)} copy(bf16[2048,1536]{1,0:T(8,128)(2,1)} %bitcast.158) | data formatting | bytes 12582912 | tf_op jit(solution)/shard_map/reshape | solution.py:98
  74.2 4.6 fusion.81
  84.8 2.7 convert_element_type.134
  88.9 2.1 copy.110
  93.2 14.6 %all-gather.11.cloned.1.call-done = bf16[1,1024,2,256]{3,1,2,0:T(8,128)(2,1)} async-done(((bf16[1,256,2,256]{3,1,2,0:T(8,128)(2,1)}), bf16[1,1024,2,256]{3,1,2,0:T(8,128)(2,1)}) %all-gather.11.cloned.1.call-update) | async-done | bytes 1048592 | tf_op jit(solution)/shard_map/all_gather | solution.py:107
  107.8 2.0 fusion.82
  110.9 15.6 %all-gather.9.cloned.1.call-done = bf16[1,1024,2,256]{3,1,2,0:T(8,128)(2,1)} async-done(((bf16[1,256,2,256]{3,1,2,0:T(8,128)(2,1)}), bf16[1,1024,2,256]{3,1,2,0:T(8,128)(2,1)}) %all-gather.9.cloned.1.call-update) | async-done | bytes 1048592 | tf_op jit(solution)/shard_map/all_gather | solution.py:108
  131.9 2.1 fusion.34
  143.3 39.8 %all-gather.15.cloned.1.call-done = bf16[2048,2048]{1,0:T(8,128)(2,1)} async-done(((bf16[256,2048]{1,0:T(8,128)(2,1)}), bf16[2048,2048]{1,0:T(8,128)(2,1)}) %all-gather.15.cloned.1.call-update) | async-done | bytes 8388624 | tf_op jit(solution)/shard_map/all_gather | solution.py:95
  183.1 7.1 convolution_add_fusion.1
  190.2 49.5 %all-gather.17.cloned.1.call-done = bf16[2048,2048]{1,0:T(8,128)(2,1)} async-done(((bf16[256,2048]{1,0:T(8,128)(2,1)}), bf16[2048,2048]{1,0:T(8,128)(2,1)}) %all-gather.17.cloned.1.call-update) | async-done | bytes 8388624 | tf_op jit(solution)/shard_map/all_gather | solution.py:142
  239.7 10.6 %fusion.78 = f32[256,2048]{1,0:T(8,128)S(1)} fusion(bf16[2048,2048]{1,0:T(8,128)(2,1)} %all-gather.17.cloned.1.call-done, f32[256,2048]{1,0:T(8,128)} %convolution_add_fusion.1), kind=kOutput, calls=%fused_computation.149 | convolution fusion | flops 2181562368 | bytes 12582912 | tf_op jit(solution)/shard_map/dot_general | solution.py:50
  250.4 2.1 convolution_add_fusion
  252.5 8.2 convert_reduce_fusion.2
  261.7 3.7 fusion.84
  265.3 8.1 reduce-scatter.5.cloned.1.call-done
  282.6 24.6 %reduce-scatter.7.cloned.1.call-done = f32[1,256,2,256]{1,3,2,0:T(8,128)} async-done(((f32[1,1024,2,256]{1,3,2,0:T(8,128)}), f32[1,256,2,256]{1,3,2,0:T(8,128)}) %reduce-scatter.7.cloned.1.call-update) | async-done | bytes 524304 | tf_op jit(solution)/shard_map/reduce_scatter | solution.py:197
  308.2 6.0 fusion.83
  317.0 6.6 convolution_bitcast_fusion
  323.6 11.0 %pad_maximum_fusion.1 = f32[2048,2560]{0,1:T(8,128)} fusion(f32[2048,2048]{0,1:T(8,128)S(1)} %convolution_bitcast_fusion, f32[2048,512]{0,1:T(8,128)S(1)} %convolution_bitcast_fusion.1), kind=kLoop, calls=%fused_computation.1 | loop fusion | flops 5242880 | bytes 41943040 | tf_op jit(solution)/shard_map/concatenate | solution.py:165
  335.3 3.8 fusion.73
  341.1 12.3 %pad_maximum_fusion = f32[2048,3584]{0,1:T(8,128)} fusion(f32[2048,2048]{0,1:T(8,128)S(1)} %fusion.73, f32[2048,1536]{0,1:T(8,128)S(1)} %fusion.50), kind=kLoop, calls=%fused_computation | loop fusion | flops 7340032 | bytes 58720256 | tf_op jit(solution)/shard_map/concatenate | solution.py:216
  353.7 183.6 %all-reduce.4.cloned.1.call-done = (f32[256,2048]{1,0:T(8,128)}, f32[256,2048]{1,0:T(8,128)}, f32[256,2048]{1,0:T(8,128)}) async-done(((f32[256,2048]{1,0:T(8,128)}, f32[256,2048]{1,0:T(8,128)}, f32[256,2048]{1,0:T(8,128)}), (f32[256,2048]{1,0:T(8,128)}, f32[256,2048]{1,0:T(8,128)}, f32[256,2048]{1,0:T(8,128)})) %all-reduce.4.cloned.1.call-update) | async-done | bytes 6291472 | tf_op jit(solution)/shard_map/psum | solution.py:148
  537.3 3.2 fusion.80
  542.5 3.3 convert_reduce_fusion.1
  545.8 24.9 %all-reduce = (f32[2,768]{1,0:T(2,128)}, f32[2048]{0:T(1024)}, f32[2048]{0:T(1024)}, f32[2048]{0:T(1024)}, f32[2048]{0:T(1024)}, /*index=5*/f32[2048]{0:T(1024)}, f32[2048]{0:T(1024)}) all-reduce(f32[2,768]{1,0:T(2,128)S(1)} %convert_reduce_fusion.3, ...), channel_id=1, replica_groups=mesh['shard'=2,'ctx'=4,'tensor'=4] {'shard','ctx'}, use_global_device_ids=true, to_apply=%region_18.19 | all-reduce | flops 13824 | bytes 110592 | tf_op jit(solution)/shard_map/psum | solution.py:233
  570.7 105.1 %reduce-scatter.11.cloned.1.call-done = f32[256,2560]{0,1:T(8,128)} async-done(((f32[2048,2560]{0,1:T(8,128)}), f32[256,2560]{0,1:T(8,128)}) %reduce-scatter.11.cloned.1.call-update) | async-done | bytes 2621456 | tf_op jit(solution)/shard_map/reduce_scatter | solution.py:164
  680.2 175.1 %reduce-scatter.9.cloned.1.call-done = f32[256,3584]{0,1:T(8,128)} async-done(((f32[2048,3584]{0,1:T(8,128)}), f32[256,3584]{0,1:T(8,128)}) %reduce-scatter.9.cloned.1.call-update) | async-done | bytes 3670032 | tf_op jit(solution)/shard_map/reduce_scatter | solution.py:215
  860.1 2.1 copy.93
  (177 shorter events, 56.2 us)
Async XLA Ops:
  7.2 4.0 copy-start.38
  7.2 5.4 copy-start
  7.2 51.4 %all-gather.7.cloned.1.call-start = ((), (), s32[]{:S(2)}) async-start(), calls=%async_computation.4 | async-start | bytes 7077888 | tf_op jit(solution)/shard_map/all_gather | solution.py:94
  10.2 78.7 %all-gather.13.cloned.1.call-start = ((), (), s32[]{:S(2)}) async-start(), calls=%async_computation.7 | async-start | bytes 2359296 | tf_op jit(solution)/shard_map/all_gather | solution.py:141
  11.2 96.6 %all-gather.11.cloned.1.call-start = ((), (), s32[]{:S(2)}) async-start(), calls=%async_computation.6 | async-start | bytes 1310720 | tf_op jit(solution)/shard_map/all_gather | solution.py:107
  12.8 61.3 %copy-start.24 = (f32[256]{0:T(256)}, f32[256]{0:T(256)S(1)}, u32[]{:S(2)}) copy-start(f32[256]{0:T(256)S(1)} %broadcast_multiply_fusion.1) | copy-start | bytes 3076
  13.3 52.1 %copy-start.28 = (f32[256]{0:T(256)}, f32[256]{0:T(256)S(1)}, u32[]{:S(2)}) copy-start(f32[256]{0:T(256)S(1)} %fusion.17) | copy-start | bytes 3076
  13.3 60.9 %copy-start.26 = (f32[256]{0:T(256)}, f32[256]{0:T(256)S(1)}, u32[]{:S(2)}) copy-start(f32[256]{0:T(256)S(1)} %fusion.67) | copy-start | bytes 3076
  65.4 8.8 %copy-start.22 = (f32[2048]{0:T(1024)S(1)}, f32[2048]{0:T(1024)}, u32[]{:S(2)}) copy-start(f32[2048]{0:T(1024)} %param.26) | copy-start | bytes 24580
  65.4 8.8 %copy-start.30 = (f32[2048]{0:T(1024)S(1)}, f32[2048]{0:T(1024)}, u32[]{:S(2)}) copy-start(f32[2048]{0:T(1024)} %param.27) | copy-start | bytes 24580
  65.4 8.8 %copy-start.40 = (f32[2,768]{1,0:T(2,128)S(1)}, f32[2,768]{1,0:T(2,128)}, u32[]{:S(2)}) copy-start(f32[2,768]{1,0:T(2,128)} %param.20) | copy-start | bytes 18436
  80.0 3.6 copy-start.11
  81.8 44.7 %all-gather.9.cloned.1.call-start = ((), (), s32[]{:S(2)}) async-start(), calls=%async_computation.5 | async-start | bytes 1310720 | tf_op jit(solution)/shard_map/all_gather | solution.py:108
  83.5 99.6 %all-gather.15.cloned.1.call-start = ((), (), s32[]{:S(2)}) async-start(), calls=%async_computation.8 | async-start | bytes 9437184 | tf_op jit(solution)/shard_map/all_gather | solution.py:95
  84.7 155.0 %all-gather.17.cloned.1.call-start = ((), (), s32[]{:S(2)}) async-start(), calls=%async_computation.9 | async-start | bytes 9437184 | tf_op jit(solution)/shard_map/all_gather | solution.py:142
  87.6 185.9 %reduce-scatter.5.cloned.1.call-start = ((), (), s32[]{:S(2)}) async-start(), calls=%async_computation.10 | async-start | bytes 2621440 | tf_op jit(solution)/shard_map/reduce_scatter | solution.py:196
  88.9 3.5 copy-start.8
  131.7 175.4 %reduce-scatter.7.cloned.1.call-start = ((), (), s32[]{:S(2)}) async-start(), calls=%async_computation.11 | async-start | bytes 2621440 | tf_op jit(solution)/shard_map/reduce_scatter | solution.py:197
  141.3 41.9 %copy-start.23 = (f32[2048]{0:T(1024)S(1)}, f32[2048]{0:T(1024)}, u32[]{:S(2)}) copy-start(f32[2048]{0:T(1024)} %param.28) | copy-start | bytes 24580
  141.3 396.0 %all-reduce.4.cloned.1.call-start = ((), (), s32[]{:S(2)}) async-start(), calls=%async_computation.14 | async-start | bytes 12582912 | tf_op jit(solution)/shard_map/psum | solution.py:148
  190.2 60.1 %copy-start.5 = (bf16[256,8,2,256]{3,1,2,0:T(8,128)(2,1)S(1)}, bf16[256,8,2,256]{3,1,2,0:T(8,128)(2,1)}, u32[]{:S(2)}) copy-start(bf16[256,8,2,256]{3,1,2,0:T(8,128)(2,1)} %copy-done.4) | copy-start | bytes 6291460
  239.7 12.7 %copy-start.39 = (bf16[2048,2048]{1,0:T(8,128)(2,1)S(1)}, bf16[2048,2048]{1,0:T(8,128)(2,1)}, u32[]{:S(2)}) copy-start(bf16[2048,2048]{1,0:T(8,128)(2,1)} %all-gather.17.cloned.1.call-done) | copy-start | bytes 25165828
  239.7 12.7 %copy-start.41 = (f32[256,2048]{1,0:T(8,128)S(1)}, f32[256,2048]{1,0:T(8,128)}, u32[]{:S(2)}) copy-start(f32[256,2048]{1,0:T(8,128)} %convolution_add_fusion.1) | copy-start | bytes 6291460
  250.4 11.3 %slice-start.4 = ((s8[8388608]{0:T(1024)(128)(4,1)}), s8[4194304]{0:T(1024)(128)(4,1)S(1)}, s32[]{:S(2)}) async-start(s8[8388608]{0:T(1024)(128)(4,1)} %bitcast.176), calls=%async_computation.19 | async-start | bytes 8388608
  252.5 9.2 %slice-start.5 = ((s8[8388608]{0:T(1024)(128)(4,1)}), s8[4194304]{0:T(1024)(128)(4,1)S(1)}, s32[]{:S(2)}) async-start(s8[8388608]{0:T(1024)(128)(4,1)} %bitcast.176), calls=%async_computation.20 | async-start | bytes 8388608
  265.3 11.4 %copy-start.7 = (f32[1,256,2,256]{3,1,2,0:T(8,128)S(1)}, f32[1,256,2,256]{3,1,2,0:T(8,128)}, u32[]{:S(2)}) copy-start(f32[1,256,2,256]{3,1,2,0:T(8,128)} %copy-done.6) | copy-start | bytes 1572868
  265.3 11.4 %copy-start.16 = (f32[1,256,2,32]{3,1,2,0:T(8,128)S(1)}, f32[1,256,2,32]{3,1,2,0:T(8,128)}, u32[]{:S(2)}) copy-start(f32[1,256,2,32]{3,1,2,0:T(8,128)} %get-tuple-element.89) | copy-start | bytes 196612
  265.3 11.4 %copy-start.17 = (f32[1,256,2,32]{3,1,2,0:T(8,128)S(1)}, f32[1,256,2,32]{3,1,2,0:T(8,128)}, u32[]{:S(2)}) copy-start(f32[1,256,2,32]{3,1,2,0:T(8,128)} %get-tuple-element.90) | copy-start | bytes 196612
  314.2 361.6 %reduce-scatter.11.cloned.1.call-start = ((), (), s32[]{:S(2)}) async-start(), calls=%async_computation.13 | async-start | bytes 23592960 | tf_op jit(solution)/shard_map/reduce_scatter | solution.py:164
  334.6 4.5 copy-start.31
  334.7 520.7 %reduce-scatter.9.cloned.1.call-start = ((), (), s32[]{:S(2)}) async-start(), calls=%async_computation.12 | async-start | bytes 33030144 | tf_op jit(solution)/shard_map/reduce_scatter | solution.py:215
  537.3 3.5 copy-start.2
  (28 other events, 47.5 us)
Sparse Core Ops, SparseCore 0:
  10.5 48.1 all-gather.6
  61.1 27.7 all-gather.12
  91.0 16.6 all-gather.10
  109.8 16.6 all-gather.8
  128.8 54.2 all-gather.14
  185.4 54.2 all-gather.16
  242.2 31.1 reduce-scatter.4
  275.9 31.1 reduce-scatter.6
  314.4 222.8 all-reduce.3
  540.7 135.0 reduce-scatter.10
  679.4 175.8 reduce-scatter.8
where the time goes:
time: 878 us; the launch traced here: 869 us
  waiting for transfers between devices  661 us (75%)
  matrix products  67.6 us (8%)
  other arithmetic  51.4 us (6%)
  local copies, waits for them, and re-layouts  47.7 us (5%)
  blocking collectives  24.9 us (3%)
  between operations  14.7 us (2%)
    psum x1, waiting for transfers between devices, local(): summed_out = lax.psum(block_out, 'tensor')  184 us
    reduce_scatter x1, waiting for transfers between devices, local(): lax.psum_scatter(jnp.concatenate([outer_rows(normed_one, grad_joined), ou...  175 us
    reduce_scatter x1, waiting for transfers between devices, local(): lax.psum_scatter(jnp.concatenate([outer_rows(grad_low, context), outer_ro...  105 us
    all_gather x1, waiting for transfers between devices, local(): lax.all_gather(fc2_low, ('shard', 'ctx'), axis=0, tiled=True)  49.5 us
    all_gather x1, waiting for transfers between devices, local(): lax.all_gather(qkv_low, ('shard', 'ctx'), axis=0, tiled=True)  45.3 us
    all_gather x1, waiting for transfers between devices, local(): lax.all_gather(fc1_low, ('shard', 'ctx'), axis=0, tiled=True)  39.8 us
    unnamed x100, local copies, waits for them, and re-layouts  24.9 us
    psum x1, blocking collectives, local(): lax.psum((bias_qkv_term, bias_fc1_term, jnp.sum(grad_flat, axis=0), grad_...  24.9 us
  transfers between devices with their start and end apart: 11, of which 10 were waited for; matrix products, arithmetic and copies ran while one was open for 16% of the time, Pallas kernels for 0%

commit v1 on v0

--- a/solution.py
+++ b/solution.py
@@ -9,6 +9,10 @@
 PIECES = 3
 EPSILON = 1e-05
 ROPE_BASE = 10000.0
+
+
+def balance_series_all_over_axis(vector):
+    return lax.all_gather(vector, axis_name="tensor").sum(axis=0)
 
 
 def layer_norm(values, norm_gain, norm_shift):
@@ -145,7 +149,7 @@
     block_out = cross_rows(context, piece_pair[0].reshape(row_span, attn_cols)) + cross_rows(
         hidden, piece_pair[1]
     )
-    summed_out = lax.psum(block_out, "tensor")
+    summed_out = balance_series_all_over_axis(block_out)
     output = (
         (residual + summed_out + out_bias)
         .astype(jnp.bfloat16)

time: 878 us -> 961 us (1.095)
  waiting for transfers between devices: 661 us -> 731 us
    all_gather x0 -> x1, waiting for transfers between devices: none -> 116 us  [balance_series_all_over_axis(): return lax.all_gather(vector, axis_name='tensor').sum(axis=0)]
    psum x1, waiting for transfers between devices: 184 us -> 101 us  [local(): lax.psum((grad_norm_one, grad_norm_two), 'tensor')]
    reduce_scatter x1, waiting for transfers between devices: 105 us -> 132 us  [local(): lax.psum_scatter(jnp.concatenate([outer_rows(grad_low, context), outer_ro...]
    reduce_scatter x1, waiting for transfers between devices: 8.08 us -> 18.4 us  [local(): lax.psum_scatter(key_terms, 'ctx', scatter_dimension=1, tiled=True)]
    unnamed x100 -> x98, local copies, waits for them, and re-layouts: 24.9 us -> 28.8 us
  transfers between devices with their start and end apart: 11 -> 12, of which waited for: 10 -> 11; matrix products, arithmetic and copies ran while one was open for 16% -> 16% of each run, Pallas kernels for 0% -> 0%
where the time goes in v1:
time: 961 us; the launch traced here: 952 us
  waiting for transfers between devices  731 us (76%)
  matrix products  68.3 us (7%)
  other arithmetic  59 us (6%)
  local copies, waits for them, and re-layouts  51.6 us (5%)
  blocking collectives  26.4 us (3%)
  between operations  15 us (2%)
    reduce_scatter x1, waiting for transfers between devices, local(): lax.psum_scatter(jnp.concatenate([outer_rows(normed_one, grad_joined), ou...  175 us
    reduce_scatter x1, waiting for transfers between devices, local(): lax.psum_scatter(jnp.concatenate([outer_rows(grad_low, context), outer_ro...  132 us
    all_gather x1, waiting for transfers between devices, balance_series_all_over_axis(): return lax.all_gather(vector, axis_name='tensor').sum(axis=0)  116 us
    psum x1, waiting for transfers between devices, local(): lax.psum((grad_norm_one, grad_norm_two), 'tensor')  101 us
    all_gather x1, waiting for transfers between devices, local(): lax.all_gather(fc2_low, ('shard', 'ctx'), axis=0, tiled=True)  49.5 us
    all_gather x1, waiting for transfers between devices, local(): lax.all_gather(qkv_low, ('shard', 'ctx'), axis=0, tiled=True)  45.3 us
    all_gather x1, waiting for transfers between devices, local(): lax.all_gather(fc1_low, ('shard', 'ctx'), axis=0, tiled=True)  41.4 us
    unnamed x98, local copies, waits for them, and re-layouts  28.8 us
  transfers between devices with their start and end apart: 12, of which 11 were waited for; matrix products, arithmetic and copies ran while one was open for 16% of the time, Pallas kernels for 0%

profile of v1, /device:TPU:0, one launch (start us, length us, event | category | flops | bytes accessed | tf_op | source)
XLA Modules:
  0.0 952.3 jit_solution(12917937584237745118)
XLA Ops:
  7.3 2.9 convert_element_type.124
  13.3 45.3 %all-gather.9.cloned.1.call-done = bf16[2048,2,768]{2,1,0:T(2,128)(2,1)} async-done(((bf16[256,2,768]{2,1,0:T(2,128)(2,1)}), bf16[2048,2,768]{2,1,0:T(2,128)(2,1)}) %all-gather.9.cloned.1.call-update) | async-done | bytes 6291472 | tf_op jit(solution)/shard_map/all_gather | solution.py:98
  58.6 6.8 copy.109
  65.4 8.8 copy.74
  74.2 4.6 fusion.79
  84.8 2.7 convert_element_type.135
  88.9 2.1 copy.110
  93.2 14.6 %all-gather.13.cloned.1.call-done = bf16[1,1024,2,256]{3,1,2,0:T(8,128)(2,1)} async-done(((bf16[1,256,2,256]{3,1,2,0:T(8,128)(2,1)}), bf16[1,1024,2,256]{3,1,2,0:T(8,128)(2,1)}) %all-gather.13.cloned.1.call-update) | async-done | bytes 1048592 | tf_op jit(solution)/shard_map/all_gather | solution.py:111
  111.0 15.6 %all-gather.11.cloned.1.call-done = bf16[1,1024,2,256]{3,1,2,0:T(8,128)(2,1)} async-done(((bf16[1,256,2,256]{3,1,2,0:T(8,128)(2,1)}), bf16[1,1024,2,256]{3,1,2,0:T(8,128)(2,1)}) %all-gather.11.cloned.1.call-update) | async-done | bytes 1048592 | tf_op jit(solution)/shard_map/all_gather | solution.py:112
  141.8 41.4 %all-gather.17.cloned.1.call-done = bf16[2048,2048]{1,0:T(8,128)(2,1)} async-done(((bf16[256,2048]{1,0:T(8,128)(2,1)}), bf16[2048,2048]{1,0:T(8,128)(2,1)}) %all-gather.17.cloned.1.call-update) | async-done | bytes 8388624 | tf_op jit(solution)/shard_map/all_gather | solution.py:99
  183.2 7.1 convolution_add_fusion.1
  190.2 49.5 %all-gather.19.cloned.1.call-done = bf16[2048,2048]{1,0:T(8,128)(2,1)} async-done(((bf16[256,2048]{1,0:T(8,128)(2,1)}), bf16[2048,2048]{1,0:T(8,128)(2,1)}) %all-gather.19.cloned.1.call-update) | async-done | bytes 8388624 | tf_op jit(solution)/shard_map/all_gather | solution.py:146
  239.7 10.6 %convert_reduce_fusion.2 = (f32[2048]{0:T(1024)}, bf16[256,2048]{1,0:T(8,128)(2,1)S(1)}) fusion(f32[256,2048]{1,0:T(8,128)} %convolution_add_fusion.1, bf16[2048,2048]{1,0:T(8,128)(2,1)} %all-gather.19.cloned.1.call-done, bf16[1,256,2048]{2,1,0:T(8,128)(2,1)} %param.16), kind=kOutput, calls=%fused_computation.41 | convolution fusion | flops 2186278912 | bytes 12591104 | tf_op jit(solution)/shard_map/dot_general | solution.py:167
  251.3 3.7 fusion.82
  255.0 18.4 %reduce-scatter.5.cloned.1.call-done = f32[1,256,2,256]{3,1,2,0:T(8,128)} async-done(((f32[1,1024,2,256]{3,1,2,0:T(8,128)}), f32[1,256,2,256]{3,1,2,0:T(8,128)}) %reduce-scatter.5.cloned.1.call-update) | async-done | bytes 524304 | tf_op jit(solution)/shard_map/reduce_scatter | solution.py:200
  276.8 2.2 fusion.53
  285.4 21.7 %reduce-scatter.7.cloned.1.call-done = f32[1,256,2,256]{1,3,2,0:T(8,128)} async-done(((f32[1,1024,2,256]{1,3,2,0:T(8,128)}), f32[1,256,2,256]{1,3,2,0:T(8,128)}) %reduce-scatter.7.cloned.1.call-update) | async-done | bytes 524304 | tf_op jit(solution)/shard_map/reduce_scatter | solution.py:201
  308.9 6.2 fusion.81
  318.0 8.7 fusion.76
  331.6 6.6 convolution_bitcast_fusion
  338.2 10.9 %pad_maximum_fusion.1 = f32[2048,2560]{0,1:T(8,128)} fusion(f32[2048,2048]{0,1:T(8,128)S(1)} %convolution_bitcast_fusion, f32[2048,512]{0,1:T(8,128)S(1)} %convolution_bitcast_fusion.1), kind=kLoop, calls=%fused_computation.1 | loop fusion | flops 5242880 | bytes 41943040 | tf_op jit(solution)/shard_map/concatenate | solution.py:169
  350.5 2.6 fusion.69
  353.0 3.1 fusion.48
  356.1 12.3 %pad_maximum_fusion = f32[2048,3584]{0,1:T(8,128)} fusion(f32[2048,2048]{0,1:T(8,128)S(1)} %fusion.69, f32[2048,1536]{0,1:T(8,128)S(1)} %fusion.48), kind=kLoop, calls=%fused_computation | loop fusion | flops 7340032 | bytes 58720256 | tf_op jit(solution)/shard_map/concatenate | solution.py:220
  369.8 100.5 %all-reduce.4.cloned.1.call-done = (f32[256,2048]{1,0:T(8,128)}, f32[256,2048]{1,0:T(8,128)}) async-done(((f32[256,2048]{1,0:T(8,128)}, f32[256,2048]{1,0:T(8,128)}), (f32[256,2048]{1,0:T(8,128)}, f32[256,2048]{1,0:T(8,128)})) %all-reduce.4.cloned.1.call-update) | async-done | bytes 4194320 | tf_op jit(solution)/shard_map/psum | solution.py:229
  470.4 3.2 fusion.78
  475.5 2.9 convert_reduce_fusion.1
  478.4 26.4 %all-reduce = (f32[2,768]{1,0:T(2,128)}, f32[2048]{0:T(1024)}, f32[2048]{0:T(1024)}, f32[2048]{0:T(1024)}, f32[2048]{0:T(1024)}, /*index=5*/f32[2048]{0:T(1024)}, f32[2048]{0:T(1024)}) all-reduce(f32[2,768]{1,0:T(2,128)S(1)} %convert_reduce_fusion.3, ...), channel_id=1, replica_groups=mesh['shard'=2,'ctx'=4,'tensor'=4] {'shard','ctx'}, use_global_device_ids=true, to_apply=%region_18.19 | all-reduce | flops 13824 | bytes 110592 | tf_op jit(solution)/shard_map/psum | solution.py:237
  504.8 116.2 %all-gather.21.cloned.1.call-done = f32[1024,2048]{1,0:T(8,128)} async-done(((f32[256,2048]{1,0:T(8,128)}), f32[1024,2048]{1,0:T(8,128)}) %all-gather.21.cloned.1.call-update) | async-done | bytes 8388624 | tf_op jit(solution)/shard_map/all_gather | solution.py:15
  621.0 4.4 reduce_sum.169
  626.7 132.3 %reduce-scatter.11.cloned.1.call-done = f32[256,2560]{0,1:T(8,128)} async-done(((f32[2048,2560]{0,1:T(8,128)}), f32[256,2560]{0,1:T(8,128)}) %reduce-scatter.11.cloned.1.call-update) | async-done | bytes 2621456 | tf_op jit(solution)/shard_map/reduce_scatter | solution.py:168
  763.3 174.9 %reduce-scatter.9.cloned.1.call-done = f32[256,3584]{0,1:T(8,128)} async-done(((f32[2048,3584]{0,1:T(8,128)}), f32[256,3584]{0,1:T(8,128)}) %reduce-scatter.9.cloned.1.call-update) | async-done | bytes 3670032 | tf_op jit(solution)/shard_map/reduce_scatter | solution.py:219
  (179 shorter events, 68.0 us)
Async XLA Ops:
  7.2 4.0 copy-start.38
  7.2 5.4 copy-start
  7.2 51.4 %all-gather.9.cloned.1.call-start = ((), (), s32[]{:S(2)}) async-start(), calls=%async_computation.4 | async-start | bytes 7077888 | tf_op jit(solution)/shard_map/all_gather | solution.py:98
  10.2 78.7 %all-gather.15.cloned.1.call-start = ((), (), s32[]{:S(2)}) async-start(), calls=%async_computation.7 | async-start | bytes 2359296 | tf_op jit(solution)/shard_map/all_gather | solution.py:145
  11.2 96.6 %all-gather.13.cloned.1.call-start = ((), (), s32[]{:S(2)}) async-start(), calls=%async_computation.6 | async-start | bytes 1310720 | tf_op jit(solution)/shard_map/all_gather | solution.py:111
  12.8 61.3 %copy-start.19 = (f32[256]{0:T(256)}, f32[256]{0:T(256)S(1)}, u32[]{:S(2)}) copy-start(f32[256]{0:T(256)S(1)} %broadcast_multiply_fusion.1) | copy-start | bytes 3076
  13.3 52.1 %copy-start.25 = (f32[256]{0:T(256)}, f32[256]{0:T(256)S(1)}, u32[]{:S(2)}) copy-start(f32[256]{0:T(256)S(1)} %fusion.21) | copy-start | bytes 3076
  13.3 60.9 %copy-start.22 = (f32[256]{0:T(256)}, f32[256]{0:T(256)S(1)}, u32[]{:S(2)}) copy-start(f32[256]{0:T(256)S(1)} %fusion.65) | copy-start | bytes 3076
  65.4 8.8 copy-start.17
  65.4 8.8 copy-start.27
  65.4 8.8 copy-start.41
  80.0 3.6 copy-start.9
  81.8 44.7 %all-gather.11.cloned.1.call-start = ((), (), s32[]{:S(2)}) async-start(), calls=%async_computation.5 | async-start | bytes 1310720 | tf_op jit(solution)/shard_map/all_gather | solution.py:112
  83.5 99.6 %all-gather.17.cloned.1.call-start = ((), (), s32[]{:S(2)}) async-start(), calls=%async_computation.8 | async-start | bytes 9437184 | tf_op jit(solution)/shard_map/all_gather | solution.py:99
  84.8 155.0 %all-gather.19.cloned.1.call-start = ((), (), s32[]{:S(2)}) async-start(), calls=%async_computation.9 | async-start | bytes 9437184 | tf_op jit(solution)/shard_map/all_gather | solution.py:146
  87.6 185.9 %reduce-scatter.5.cloned.1.call-start = ((), (), s32[]{:S(2)}) async-start(), calls=%async_computation.10 | async-start | bytes 2621440 | tf_op jit(solution)/shard_map/reduce_scatter | solution.py:200
  88.9 3.5 copy-start.7
  131.7 175.4 %reduce-scatter.7.cloned.1.call-start = ((), (), s32[]{:S(2)}) async-start(), calls=%async_computation.11 | async-start | bytes 2621440 | tf_op jit(solution)/shard_map/reduce_scatter | solution.py:201
  139.7 43.4 %copy-start.18 = (f32[2048]{0:T(1024)S(1)}, f32[2048]{0:T(1024)}, u32[]{:S(2)}) copy-start(f32[2048]{0:T(1024)} %param.28) | copy-start | bytes 24580
  139.7 43.4 %copy-start.20 = (f32[256]{0:T(256)S(1)}, f32[256]{0:T(256)}, u32[]{:S(2)}) copy-start(f32[256]{0:T(256)} %copy-done.19) | copy-start | bytes 3076
  139.7 43.4 %copy-start.23 = (f32[256]{0:T(256)S(1)}, f32[256]{0:T(256)}, u32[]{:S(2)}) copy-start(f32[256]{0:T(256)} %copy-done.22) | copy-start | bytes 3076
  139.7 43.4 %copy-start.29 = (f32[2048]{0:T(1024)S(1)}, f32[2048]{0:T(1024)}, u32[]{:S(2)}) copy-start(f32[2048]{0:T(1024)} %param.29) | copy-start | bytes 24580
  139.7 43.4 %copy-start.40 = (f32[2048]{0:T(1024)S(1)}, f32[2048]{0:T(1024)}, u32[]{:S(2)}) copy-start(f32[2048]{0:T(1024)} %param.23) | copy-start | bytes 24580
  141.7 328.6 %all-reduce.4.cloned.1.call-start = ((), (), s32[]{:S(2)}) async-start(), calls=%async_computation.15 | async-start | bytes 8388608 | tf_op jit(solution)/shard_map/psum | solution.py:229
  239.7 11.6 %copy-start.39 = (bf16[2048,2048]{1,0:T(8,128)(2,1)S(1)}, bf16[2048,2048]{1,0:T(8,128)(2,1)}, u32[]{:S(2)}) copy-start(bf16[2048,2048]{1,0:T(8,128)(2,1)} %all-gather.17.cloned.1.call-done) | copy-start | bytes 25165828
  315.2 305.8 %all-gather.21.cloned.1.call-start = ((), (), s32[]{:S(2)}) async-start(), calls=%async_computation.14 | async-start | bytes 10485760 | tf_op jit(solution)/shard_map/all_gather | solution.py:15
  317.9 8.7 copy-start.5
  328.8 430.1 %reduce-scatter.11.cloned.1.call-start = ((), (), s32[]{:S(2)}) async-start(), calls=%async_computation.13 | async-start | bytes 23592960 | tf_op jit(solution)/shard_map/reduce_scatter | solution.py:168
  349.2 3.8 copy-start.28
  349.2 589.0 %reduce-scatter.9.cloned.1.call-start = ((), (), s32[]{:S(2)}) async-start(), calls=%async_computation.12 | async-start | bytes 33030144 | tf_op jit(solution)/shard_map/reduce_scatter | solution.py:219
  470.3 3.5 copy-start.2
  621.0 4.4 copy-start.31
  (28 other events, 44.6 us)
Sparse Core Ops, SparseCore 0:
  10.5 48.1 all-gather.8
  61.1 27.7 all-gather.14
  91.1 16.6 all-gather.12
  109.8 16.6 all-gather.10
  128.8 54.2 all-gather.16
  185.4 54.2 all-gather.18
  242.3 31.1 reduce-scatter.4
  276.0 31.1 reduce-scatter.6
  315.3 155.0 all-reduce.3
  472.3 148.5 all-gather.20
  624.6 134.3 reduce-scatter.10
  762.4 175.8 reduce-scatter.8
